TPU v7x, 32 devices: a whole 2x2x4 slice. The times are simulated.
32 devices in a mesh: dp: 4 (over y, core), seq: 8 (over z, x).
Axes of the slice: x: 2, y: 2, z: 4, core: 2. Of those that a mesh axis runs over, the one named last changes fastest.
Arguments:
- layer_input: bfloat16 [4096, 8192], P(('dp', 'seq')), may hold values from -6 to 6
- queries: bfloat16 [4096, 4096], P(('dp', 'seq')), may hold values from -110 to 110, as said below
- key_states: bfloat16 [4096, 512], P(('dp', 'seq')), may hold values from -12 to 12, as said below
- value_states: bfloat16 [4096, 512], P(('dp', 'seq')), may hold values from -6 to 6
- out_grad: bfloat16 [4096, 4096], P(('dp', 'seq')), may hold values from -6 to 6
Outputs:
- query_grad: bfloat16 [4096, 4096], P(('dp', 'seq'))
- key_grad: bfloat16 [4096, 512], P(('dp', 'seq'))
- value_grad: bfloat16 [4096, 512], P(('dp', 'seq'))
- weight_grad: float32 [8192, 1024], P(('dp', 'seq'))
Inputs may be any that keep to these rules, and one draw needn't show every extreme that they name: `queries`: rows of rough scales; some queries may nearly coincide in direction with keys of earlier positions. `key_states`: rows of rough scales.
All inputs are finite; a program needn't handle non-finite values.
Results may differ from a plain program's by a relative error of at most 0.0051.
Values may be sent and summed in bfloat16 or wider, within the bound.
No kernel may reach another device: no remote copies, remote signals or barrier semaphores. Data moves between devices by JAX's collectives and lax.ppermute only.
A program may use at most 128 MiB of HBM per device.

v0:
```python
import math
import jax
import jax.numpy as jnp
from jax import lax
from jax.sharding import PartitionSpec as P

D = 8192
QH = 32
KVH = 4
HD = 128
NEGATIVE = -1e30


def local(layer_input, queries, key_states, value_states, out_grad):
    local_rows = layer_input.shape[0]
    cycle_size = lax.axis_size("seq")
    replicas = lax.axis_size("dp")
    position = lax.axis_index("seq")
    length = local_rows * cycle_size
    group = QH // KVH
    channels = KVH * HD
    scale = 1.0 / math.sqrt(HD)
    block = math.gcd(length, 512)
    key_all, value_all = (
        lax.all_gather(key_states, "seq", axis=0, tiled=True),
        lax.all_gather(value_states, "seq", axis=0, tiled=True),
    )
    query_heads = queries.reshape(local_rows, KVH, group, HD)
    grad_heads = out_grad.reshape(local_rows, KVH, group, HD)
    query_place = position * local_rows + jnp.arange(local_rows, dtype=jnp.int32)
    needed = (position * local_rows + local_rows + block - 1) // block

    def block_scores(begin):
        key_block = lax.dynamic_slice_in_dim(key_all, begin, block, 0).reshape(block, KVH, HD)
        value_block = lax.dynamic_slice_in_dim(value_all, begin, block, 0).reshape(block, KVH, HD)
        scores = (
            jnp.einsum("tkgd,skd->kgts", query_heads, key_block, preferred_element_type=jnp.float32)
            * scale
        )
        key_place = begin + jnp.arange(block, dtype=jnp.int32)
        visible = key_place[None, :] <= query_place[:, None]
        scores = jnp.where(visible, scores, NEGATIVE)
        grad_probs = jnp.einsum(
            "tkgd,skd->kgts", grad_heads, value_block, preferred_element_type=jnp.float32
        )
        return (key_block, scores, grad_probs)

    def first_pass(step_index, carry):
        row_max, denom, weighted = carry
        key_block, scores, grad_probs = block_scores(step_index * block)
        new_max = jnp.maximum(row_max, jnp.max(scores, axis=-1))
        factor = jnp.exp(row_max - new_max)
        expon = jnp.exp(scores - new_max[..., None])
        return (
            new_max,
            denom * factor + jnp.sum(expon, axis=-1),
            weighted * factor + jnp.sum(expon * grad_probs, axis=-1),
        )

    stats_shape = (KVH, group, local_rows)
    start_stats = (
        jnp.full(stats_shape, NEGATIVE, jnp.float32),
        jnp.zeros(stats_shape, jnp.float32),
        jnp.zeros(stats_shape, jnp.float32),
    )
    row_max, denom, weighted = lax.fori_loop(0, needed, first_pass, start_stats)
    delta = weighted / denom

    def second_pass(step_index, carry):
        grad_query, terms = carry
        begin = step_index * block
        key_block, scores, grad_probs = block_scores(begin)
        probs = jnp.exp(scores - row_max[..., None]) / denom[..., None]
        grad_scores = (scale * probs * (grad_probs - delta[..., None])).astype(jnp.bfloat16)
        probs_low = probs.astype(jnp.bfloat16)
        grad_query = grad_query + jnp.einsum(
            "kgts,skd->tkgd", grad_scores, key_block, preferred_element_type=jnp.float32
        )
        key_part = jnp.einsum(
            "kgts,tkgd->skd", grad_scores, query_heads, preferred_element_type=jnp.float32
        )
        value_part = jnp.einsum(
            "kgts,tkgd->skd", probs_low, grad_heads, preferred_element_type=jnp.float32
        )
        joined = jnp.concatenate(
            [key_part.reshape(block, channels), value_part.reshape(block, channels)], axis=1
        )
        terms = lax.dynamic_update_slice_in_dim(terms, joined, begin, 0)
        return (grad_query, terms)

    start_grads = (
        jnp.zeros((local_rows, KVH, group, HD), jnp.float32),
        jnp.zeros((length, 2 * channels), jnp.float32),
    )
    grad_query, terms = lax.fori_loop(0, needed, second_pass, start_grads)
    query_grad = grad_query.reshape(local_rows, QH * HD).astype(jnp.bfloat16)
    owned_grads = lax.psum_scatter(terms, "seq", scatter_dimension=0, tiled=True).astype(
        jnp.bfloat16
    )
    summed_grads = lax.all_gather(owned_grads, "seq", axis=0, tiled=True)
    slab = D // (replicas * cycle_size)
    columns = lax.all_to_all(
        layer_input.reshape(local_rows, replicas, cycle_size, slab),
        "seq",
        split_axis=2,
        concat_axis=0,
        tiled=True,
    )
    columns = columns.reshape(length, replicas * slab)
    weight_grad = lax.psum_scatter(
        jnp.einsum("tr,tc->rc", columns, summed_grads, preferred_element_type=jnp.float32),
        "dp",
        scatter_dimension=0,
        tiled=True,
    )
    return (query_grad, owned_grads[:, :channels], owned_grads[:, channels:], weight_grad)


def solution(mesh):
    in_specs = (
        P(("dp", "seq"), None),
        P(("dp", "seq"), None),
        P(("dp", "seq"), None),
        P(("dp", "seq"), None),
        P(("dp", "seq"), None),
    )
    out_specs = (
        P(("dp", "seq"), None),
        P(("dp", "seq"), None),
        P(("dp", "seq"), None),
        P(("dp", "seq"), None),
    )
    return jax.shard_map(local, mesh=mesh, in_specs=in_specs, out_specs=out_specs, check_vma=False)
```

profile of v0, /device:TPU:0, one launch (start us, length us, event | category | flops | bytes accessed | tf_op | source)
XLA Modules:
  0.0 388.9 jit_solution(6068416372018879133)
XLA Ops:
  7.2 1.7 copy.69
  8.9 1.7 copy.71
  10.7 1.6 copy.70
  13.0 1.6 copy.72
  15.9 37.0 %all-gather.4.cloned.1.call-done = bf16[1024,512]{0,1:T(8,128)(2,1)} async-done(((bf16[128,512]{0,1:T(8,128)(2,1)}), bf16[1024,512]{0,1:T(8,128)(2,1)}) %all-gather.4.cloned.1.call-update) | async-done | bytes 1048592 | tf_op jit(solution)/shard_map/all_gather | solution.py:25
  52.9 41.1 %all-gather.6.cloned.1.call-done = bf16[1024,512]{0,1:T(8,128)(2,1)} async-done(((bf16[128,512]{0,1:T(8,128)(2,1)}), bf16[1024,512]{0,1:T(8,128)(2,1)}) %all-gather.6.cloned.1.call-update) | async-done | bytes 1048592 | tf_op jit(solution)/shard_map/all_gather | solution.py:26
  94.0 7.5 %while.28 = (s32[]{:T(128)}, f32[4,8,128]{2,1,0:T(8,128)S(1)}, f32[4,8,128]{2,1,0:T(8,128)S(1)}, f32[4,8,128]{2,1,0:T(8,128)S(1)}, s32[]{:T(128)}, /*index=5*/bf...) while((s32[]{:T(128)}, f32[4,8,128]{2,1,0:T(8,128)S(1)}, ...), condition=%wide.region_4.5_spmd.clone, body=%wide.region_0.4_spmd.clone.sunk | while | flops 1098986112 | bytes 35165400 | solution.py:66
  96.9 1.8 fusion.59
  98.7 2.7 fusion.58
  101.5 2.5 broadcast_in_dim.32.clone
  104.0 1.6 broadcast_in_dim.31
  105.6 19.8 %while.29 = (s32[]{:T(128)}, f32[128,4,8,128]{0,3,2,1:T(8,128)}, f32[1024,1024]{1,0:T(8,128)}, s32[]{:T(128)}, bf16[1024,512]{0,1:T(8,128)(2,1)}, /*index=5*/bf1...) while((s32[]{:T(128)}, f32[128,4,8,128]{0,3,2,1:T(8,128)}, ...), condition=%wide.region_6.7_spmd.clone, body=%wide.region_5.6_spmd.clone.sunk | while | flops 2704343552 | bytes 108713312 | solution.py:95
  105.6 1.6 constant_dynamic-slice_fusion.7
  107.4 2.3 fusion.70
  109.8 1.7 fusion.71
  111.5 1.5 fusion.73
  113.4 1.5 fusion.72
  114.9 1.5 pad_maximum_fusion.2
  116.4 1.9 copy.110
  118.4 1.5 constant_dynamic-update-slice_fusion.2
  121.3 4.1 %bitcast_add_fusion.2 = f32[128,4,8,128]{0,3,2,1:T(8,128)} fusion(f32[128,4,8,128]{0,3,2,1:T(8,128)} %get-tuple-element.501, bf16[512,4,128,1]{0,2,3,1:T(8,128)(2,1)} %bitcast.153, bf16[4,8,128,512]{2,3,1,0:T(8,128)(2,1)S(1)} %copy-done.1), kind=kOutput, calls=%fused_computation.26.clone.1 | convolution fusion | flops 537395200 | bytes 8912896 | tf_op jit(solution)/shard_map/while/body/kgts,skd->tkgd/dot_general | solution.py:76
  125.4 3.2 copy.77
  128.6 1.5 copy.78
  130.1 30.8 %all-to-all-start = ((bf16[128,4,8,256]{0,3,1,2:T(8,128)(2,1)}), bf16[128,4,8,256]{0,3,1,2:T(8,128)(2,1)S(1)}, u32[]{:S(2)}, u32[]{:S(2)}) async-start(bf16[128,4,8,256]{0,3,1,2:T(8,128)(2,1)} %copy.78), calls=%async_computation.1 | async-start | bytes 4194304 | tf_op jit(solution)/shard_map/all_to_all | solution.py:102
  161.0 117.2 %reduce-scatter.3.cloned.1.call-done = f32[128,1024]{1,0:T(8,128)} async-done(((f32[1024,1024]{1,0:T(8,128)}), f32[128,1024]{1,0:T(8,128)}) %reduce-scatter.3.cloned.1.call-update) | async-done | bytes 524304 | tf_op jit(solution)/shard_map/reduce_scatter | solution.py:97
  278.2 1.8 convert_element_type.17
  280.3 2.7 copy.79
  283.0 47.1 %all-gather.8.cloned.1.call-done = bf16[1024,1024]{1,0:T(8,128)(2,1)} async-done(((bf16[128,1024]{1,0:T(8,128)(2,1)}), bf16[1024,1024]{1,0:T(8,128)(2,1)}) %all-gather.8.cloned.1.call-update) | async-done | bytes 2097168 | tf_op jit(solution)/shard_map/all_gather | solution.py:100
  330.0 6.6 %convolution_bitcast_fusion = f32[1024,1024]{0,1:T(8,128)} fusion(bf16[1024,1024]{1,0:T(8,128)(2,1)} %all-gather.8.cloned.1.call-done, bf16[128,8,8,128]{3,2,1,0:T(8,128)(2,1)} %bitcast.159), kind=kOutput, calls=%fused_computation.33 | convolution fusion | flops 2147483648 | bytes 8388608 | tf_op jit(solution)/shard_map/tr,tc->rc/dot_general | solution.py:111
  336.6 1.6 copy-done.2
  340.4 39.4 %reduce-scatter.5.cloned.1.call-done = f32[256,1024]{0,1:T(8,128)} async-done(((f32[1024,1024]{0,1:T(8,128)}), f32[256,1024]{0,1:T(8,128)}) %reduce-scatter.5.cloned.1.call-update) | async-done | bytes 1048592 | tf_op jit(solution)/shard_map/reduce_scatter | solution.py:110
  379.8 2.5 copy.80
  (46 shorter events, 9.7 us)
Async XLA Ops:
  7.2 45.7 %all-gather.4.cloned.1.call-start = ((), (), s32[]{:S(2)}) async-start(), calls=%async_computation.3 | async-start | bytes 1179648 | tf_op jit(solution)/shard_map/all_gather | solution.py:25
  8.9 85.1 %all-gather.6.cloned.1.call-start = ((), (), s32[]{:S(2)}) async-start(), calls=%async_computation.4 | async-start | bytes 1179648 | tf_op jit(solution)/shard_map/all_gather | solution.py:26
  10.6 267.5 %reduce-scatter.3.cloned.1.call-start = ((), (), s32[]{:S(2)}) async-start(), calls=%async_computation.5 | async-start | bytes 4718592 | tf_op jit(solution)/shard_map/reduce_scatter | solution.py:97
  96.9 1.8 copy-start.7
  105.6 5.8 %copy-start.3 = (bf16[128,4,8,128]{0,3,2,1:T(8,128)(2,1)}, bf16[128,4,8,128]{0,3,2,1:T(8,128)(2,1)S(1)}, u32[]{:S(2)}) copy-start(bf16[128,4,8,128]{0,3,2,1:T(8,128)(2,1)S(1)} %get-tuple-element.521) | copy-start | bytes 3145732 | tf_op jit(solution)/shard_map/while
  107.2 2.5 copy-start.5
  111.5 2.0 copy-start
  118.3 2.9 copy-start.1
  121.3 4.1 %copy-start.4 = (bf16[128,4,8,128]{0,3,2,1:T(8,128)(2,1)S(1)}, bf16[128,4,8,128]{0,3,2,1:T(8,128)(2,1)}, u32[]{:S(2)}) copy-start(bf16[128,4,8,128]{0,3,2,1:T(8,128)(2,1)} %copy-done.3) | copy-start | bytes 3145732 | tf_op jit(solution)/shard_map/while
  130.1 150.1 %all-to-all-start = ((bf16[128,4,8,256]{0,3,1,2:T(8,128)(2,1)}), bf16[128,4,8,256]{0,3,1,2:T(8,128)(2,1)S(1)}, u32[]{:S(2)}, u32[]{:S(2)}) async-start(bf16[128,4,8,256]{0,3,1,2:T(8,128)(2,1)} %copy.78), calls=%async_computation.1 | async-start | bytes 4194304 | tf_op jit(solution)/shard_map/all_to_all | solution.py:102
  160.9 169.1 %all-gather.8.cloned.1.call-start = ((), (), s32[]{:S(2)}) async-start(), calls=%async_computation.6 | async-start | bytes 2359296 | tf_op jit(solution)/shard_map/all_gather | solution.py:100
  280.0 99.8 %reduce-scatter.5.cloned.1.call-start = ((), (), s32[]{:S(2)}) async-start(), calls=%async_computation.7 | async-start | bytes 5242880 | tf_op jit(solution)/shard_map/reduce_scatter | solution.py:110
  336.6 1.6 copy-start.2
  336.6 3.1 copy-start.6
Sparse Core Ops, SparseCore 0:
  10.6 42.2 all-gather.3
  55.5 38.4 all-gather.5
  125.5 152.5 reduce-scatter.2
  280.9 49.0 all-gather.7
  336.8 42.9 reduce-scatter.4
where the time goes:
time: 390 us; the launch traced here: 389 us
  waiting for transfers between devices  282 us (72%)
  local copies, waits for them, and re-layouts  34.5 us (9%)
  starting transfers between devices  31.2 us (8%)
  matrix products  21.8 us (6%)
  between operations  13.9 us (4%)
  other arithmetic  5.56 us (1%)
    reduce_scatter x1, waiting for transfers between devices, local(): lax.psum_scatter(terms, 'seq', scatter_dimension=0, tiled=True)  117 us
    all_gather x1, waiting for transfers between devices, local(): summed_grads = lax.all_gather(owned_grads, 'seq', axis=0, tiled=True)  47.1 us
    all_gather x1, waiting for transfers between devices, local(): lax.all_gather(value_states, 'seq', axis=0, tiled=True)  41.1 us
    reduce_scatter x1, waiting for transfers between devices, local(): lax.psum_scatter(jnp.einsum('tr,tc->rc', columns, summed_grads, preferred...  39.4 us
    all_gather x1, waiting for transfers between devices, local(): lax.all_gather(key_states, 'seq', axis=0, tiled=True)  37 us
    all_to_all x1, starting transfers between devices, local(): lax.all_to_all(layer_input.reshape(local_rows, replicas, cycle_size, slab...  30.8 us
    unnamed x12, local copies, waits for them, and re-layouts  15.9 us
  transfers between devices with their start and end apart: 6, of which 5 were waited for; matrix products, arithmetic and copies ran while one was open for 5% of the time, Pallas kernels for 0%

commit v1 on v0

--- a/solution.py
+++ b/solution.py
@@ -9,6 +9,17 @@
 KVH = 4
 HD = 128
 NEGATIVE = -1e30
+
+
+def pass_along(array, name, d):
+    peers = lax.axis_size(name)
+    hops = [(i, (i + 1) % peers) for i in range(peers)]
+    parts = [array]
+    for far in range(1, peers):
+        parts = [lax.ppermute(parts[0], name, hops), *parts]
+    result = jnp.concatenate(parts, axis=d)
+    shift = (lax.axis_index(name) + 1) * parts[-1].shape[d]
+    return jnp.roll(result, shift, axis=d)
 
 
 def local(layer_input, queries, key_states, value_states, out_grad):
@@ -97,7 +108,7 @@
     owned_grads = lax.psum_scatter(terms, "seq", scatter_dimension=0, tiled=True).astype(
         jnp.bfloat16
     )
-    summed_grads = lax.all_gather(owned_grads, "seq", axis=0, tiled=True)
+    summed_grads = pass_along(owned_grads, "seq", 0)
     slab = D // (replicas * cycle_size)
     columns = lax.all_to_all(
         layer_input.reshape(local_rows, replicas, cycle_size, slab),

time: 390 us -> 410 us (1.051)
  waiting for transfers between devices: 282 us -> 298 us
  local copies, waits for them, and re-layouts: 34.5 us -> 39.4 us
    ppermute x0 -> x7, waiting for transfers between devices: none -> 64.4 us  [pass_along(): parts = [lax.ppermute(parts[0], name, hops), *parts]]
    all_gather x1 -> x0, waiting for transfers between devices: 47.1 us -> none  [local(): summed_grads = lax.all_gather(owned_grads, 'seq', axis=0, tiled=True)]
    unnamed x12 -> x38, local copies, waits for them, and re-layouts: 15.9 us -> 22.1 us
  transfers between devices with their start and end apart: 6 -> 12, of which waited for: 5 -> 11; matrix products, arithmetic and copies ran while one was open for 5% -> 4% of each run, Pallas kernels for 0% -> 0%
where the time goes in v1:
time: 410 us; the launch traced here: 409 us
  waiting for transfers between devices  298 us (73%)
  local copies, waits for them, and re-layouts  39.4 us (10%)
  starting transfers between devices  32.6 us (8%)
  matrix products  19.6 us (5%)
  between operations  14 us (3%)
  other arithmetic  4.99 us (1%)
    reduce_scatter x1, waiting for transfers between devices, local(): lax.psum_scatter(terms, 'seq', scatter_dimension=0, tiled=True)  117 us
    ppermute x7, waiting for transfers between devices, pass_along(): parts = [lax.ppermute(parts[0], name, hops), *parts]  64.4 us
    all_gather x1, waiting for transfers between devices, local(): lax.all_gather(value_states, 'seq', axis=0, tiled=True)  41.1 us
    reduce_scatter x1, waiting for transfers between devices, local(): lax.psum_scatter(jnp.einsum('tr,tc->rc', columns, summed_grads, preferred...  38.1 us
    all_gather x1, waiting for transfers between devices, local(): lax.all_gather(key_states, 'seq', axis=0, tiled=True)  37 us
    all_to_all x1, starting transfers between devices, local(): lax.all_to_all(layer_input.reshape(local_rows, replicas, cycle_size, slab...  30.9 us
    unnamed x38, local copies, waits for them, and re-layouts  22.1 us
  transfers between devices with their start and end apart: 12, of which 11 were waited for; matrix products, arithmetic and copies ran while one was open for 4% of the time, Pallas kernels for 0%

profile of v1, /device:TPU:0, one launch (start us, length us, event | category | flops | bytes accessed | tf_op | source)
XLA Modules:
  0.0 408.8 jit_solution(1612613472445662216)
XLA Ops:
  7.2 1.7 copy.69
  8.9 1.7 copy.71
  10.7 1.6 copy.70
  13.0 1.6 copy.72
  15.9 37.0 %all-gather.3.cloned.1.call-done = bf16[1024,512]{0,1:T(8,128)(2,1)} async-done(((bf16[128,512]{0,1:T(8,128)(2,1)}), bf16[1024,512]{0,1:T(8,128)(2,1)}) %all-gather.3.cloned.1.call-update) | async-done | bytes 1048592 | tf_op jit(solution)/shard_map/all_gather | solution.py:36
  52.9 41.1 %all-gather.5.cloned.1.call-done = bf16[1024,512]{0,1:T(8,128)(2,1)} async-done(((bf16[128,512]{0,1:T(8,128)(2,1)}), bf16[1024,512]{0,1:T(8,128)(2,1)}) %all-gather.5.cloned.1.call-update) | async-done | bytes 1048592 | tf_op jit(solution)/shard_map/all_gather | solution.py:37
  94.0 7.5 %while.28 = (s32[]{:T(128)}, f32[4,8,128]{2,1,0:T(8,128)S(1)}, f32[4,8,128]{2,1,0:T(8,128)S(1)}, f32[4,8,128]{2,1,0:T(8,128)S(1)}, s32[]{:T(128)}, /*index=5*/bf...) while((s32[]{:T(128)}, f32[4,8,128]{2,1,0:T(8,128)S(1)}, ...), condition=%wide.region_4.5_spmd.clone, body=%wide.region_0.4_spmd.clone.sunk | while | flops 1098986112 | bytes 35165400 | solution.py:77
  96.9 1.8 fusion.60
  98.7 2.7 fusion.59
  101.5 2.5 broadcast_in_dim.32.clone
  104.0 1.6 broadcast_in_dim.31
  105.6 19.9 %while.29 = (s32[]{:T(128)}, f32[128,4,8,128]{0,3,2,1:T(8,128)}, f32[1024,1024]{1,0:T(8,128)}, s32[]{:T(128)}, bf16[1024,512]{0,1:T(8,128)(2,1)}, /*index=5*/bf1...) while((s32[]{:T(128)}, f32[128,4,8,128]{0,3,2,1:T(8,128)}, ...), condition=%wide.region_6.7_spmd.clone, body=%wide.region_5.6_spmd.clone.sunk | while | flops 2704343552 | bytes 108713312 | solution.py:106
  105.6 1.6 constant_dynamic-slice_fusion.7
  107.4 2.3 fusion.71
  109.8 1.7 fusion.72
  116.5 1.9 copy.110
  121.3 4.1 %bitcast_add_fusion.2 = f32[128,4,8,128]{0,3,2,1:T(8,128)} fusion(f32[128,4,8,128]{0,3,2,1:T(8,128)} %get-tuple-element.501, bf16[512,4,128,1]{0,2,3,1:T(8,128)(2,1)} %bitcast.152, bf16[4,8,128,512]{2,3,1,0:T(8,128)(2,1)S(1)} %copy-done.1), kind=kOutput, calls=%fused_computation.26.clone.1 | convolution fusion | flops 537395200 | bytes 8912896 | tf_op jit(solution)/shard_map/while/body/kgts,skd->tkgd/dot_general | solution.py:87
  125.5 3.2 copy.77
  130.2 30.9 %all-to-all-start = ((bf16[128,4,8,256]{0,3,1,2:T(8,128)(2,1)}), bf16[128,4,8,256]{0,3,1,2:T(8,128)(2,1)S(1)}, u32[]{:S(2)}, u32[]{:S(2)}) async-start(bf16[128,4,8,256]{0,3,1,2:T(8,128)(2,1)} %copy.78), calls=%async_computation.1 | async-start | bytes 4194304 | tf_op jit(solution)/shard_map/all_to_all | solution.py:113
  161.1 117.5 %reduce-scatter.3.cloned.1.call-done = f32[128,1024]{1,0:T(8,128)} async-done(((f32[1024,1024]{1,0:T(8,128)}), f32[128,1024]{1,0:T(8,128)}) %reduce-scatter.3.cloned.1.call-update) | async-done | bytes 524304 | tf_op jit(solution)/shard_map/reduce_scatter | solution.py:108
  279.7 1.5 collective-permute-start
  281.3 9.3 %collective-permute-done = bf16[128,1024]{1,0:T(8,128)(2,1)S(1)} collective-permute-done((bf16[128,1024]{1,0:T(8,128)(2,1)S(1)}, bf16[128,1024]{1,0:T(8,128)(2,1)S(1)}, u32[]{:S(2)}, u32[]{:S(2)}) %collective-permute-start) | collective-permute-done | bytes 262176 | tf_op jit(solution)/shard_map/ppermute | solution.py:19
  290.6 9.9 %collective-permute-done.1 = bf16[128,1024]{1,0:T(8,128)(2,1)S(1)} collective-permute-done((bf16[128,1024]{1,0:T(8,128)(2,1)S(1)}, bf16[128,1024]{1,0:T(8,128)(2,1)S(1)}, u32[]{:S(2)}, u32[]{:S(2)}) %collective-permute-start.1) | collective-permute-done | bytes 262176 | tf_op jit(solution)/shard_map/ppermute | solution.py:19
  300.5 9.1 %collective-permute-done.2 = bf16[128,1024]{1,0:T(8,128)(2,1)S(1)} collective-permute-done((bf16[128,1024]{1,0:T(8,128)(2,1)S(1)}, bf16[128,1024]{1,0:T(8,128)(2,1)S(1)}, u32[]{:S(2)}, u32[]{:S(2)}) %collective-permute-start.2) | collective-permute-done | bytes 262176 | tf_op jit(solution)/shard_map/ppermute | solution.py:19
  310.3 9.1 %collective-permute-done.3 = bf16[128,1024]{1,0:T(8,128)(2,1)S(1)} collective-permute-done((bf16[128,1024]{1,0:T(8,128)(2,1)S(1)}, bf16[128,1024]{1,0:T(8,128)(2,1)S(1)}, u32[]{:S(2)}, u32[]{:S(2)}) %collective-permute-start.3) | collective-permute-done | bytes 262176 | tf_op jit(solution)/shard_map/ppermute | solution.py:19
  320.0 9.1 %collective-permute-done.4 = bf16[128,1024]{1,0:T(8,128)(2,1)S(1)} collective-permute-done((bf16[128,1024]{1,0:T(8,128)(2,1)S(1)}, bf16[128,1024]{1,0:T(8,128)(2,1)S(1)}, u32[]{:S(2)}, u32[]{:S(2)}) %collective-permute-start.4) | collective-permute-done | bytes 262176 | tf_op jit(solution)/shard_map/ppermute | solution.py:19
  329.8 10.0 %collective-permute-done.5 = bf16[128,1024]{1,0:T(8,128)(2,1)} collective-permute-done((bf16[128,1024]{1,0:T(8,128)(2,1)S(1)}, bf16[128,1024]{1,0:T(8,128)(2,1)}, u32[]{:S(2)}, u32[]{:S(2)}) %collective-permute-start.5) | collective-permute-done | bytes 262176 | tf_op jit(solution)/shard_map/ppermute | solution.py:19
  341.2 8.0 %collective-permute-done.6 = bf16[128,1024]{1,0:T(8,128)(2,1)} collective-permute-done((bf16[128,1024]{1,0:T(8,128)(2,1)}, bf16[128,1024]{1,0:T(8,128)(2,1)}, u32[]{:S(2)}, u32[]{:S(2)}) %collective-permute-start.6) | collective-permute-done | bytes 262176 | tf_op jit(solution)/shard_map/ppermute | solution.py:19
  353.5 4.3 %convolution_bitcast_fusion = f32[1024,1024]{0,1:T(8,128)} fusion(bf16[128,8,8,128]{3,2,1,0:T(8,128)(2,1)S(1)} %bitcast.158, bf16[2048,1024]{1,0:T(8,128)(2,1)S(1)} %constant_dynamic-update-slice_fusion.1, s32[]{:T(128)S(6)} %select_n.35), kind=kOutput, calls=%fused_computation.33 | convolution fusion | flops 2147483648 | bytes 8388612 | tf_op jit(solution)/shard_map/tr,tc->rc/dot_general | solution.py:122
  357.8 1.6 copy-done.2
  361.6 38.1 %reduce-scatter.5.cloned.1.call-done = f32[256,1024]{0,1:T(8,128)} async-done(((f32[1024,1024]{0,1:T(8,128)}), f32[256,1024]{0,1:T(8,128)}) %reduce-scatter.5.cloned.1.call-update) | async-done | bytes 1048592 | tf_op jit(solution)/shard_map/reduce_scatter | solution.py:121
  399.7 2.5 copy.80
  (85 shorter events, 25.6 us)
Async XLA Ops:
  7.2 45.7 %all-gather.3.cloned.1.call-start = ((), (), s32[]{:S(2)}) async-start(), calls=%async_computation.3 | async-start | bytes 1179648 | tf_op jit(solution)/shard_map/all_gather | solution.py:36
  8.9 85.1 %all-gather.5.cloned.1.call-start = ((), (), s32[]{:S(2)}) async-start(), calls=%async_computation.4 | async-start | bytes 1179648 | tf_op jit(solution)/shard_map/all_gather | solution.py:37
  10.6 267.9 %reduce-scatter.3.cloned.1.call-start = ((), (), s32[]{:S(2)}) async-start(), calls=%async_computation.5 | async-start | bytes 4718592 | tf_op jit(solution)/shard_map/reduce_scatter | solution.py:108
  96.9 1.8 copy-start.7
  105.6 5.8 %copy-start.3 = (bf16[128,4,8,128]{0,3,2,1:T(8,128)(2,1)}, bf16[128,4,8,128]{0,3,2,1:T(8,128)(2,1)S(1)}, u32[]{:S(2)}) copy-start(bf16[128,4,8,128]{0,3,2,1:T(8,128)(2,1)S(1)} %get-tuple-element.521) | copy-start | bytes 3145732 | tf_op jit(solution)/shard_map/while
  107.2 2.5 copy-start.5
  111.5 2.0 copy-start
  118.4 2.9 copy-start.1
  121.3 4.1 %copy-start.4 = (bf16[128,4,8,128]{0,3,2,1:T(8,128)(2,1)S(1)}, bf16[128,4,8,128]{0,3,2,1:T(8,128)(2,1)}, u32[]{:S(2)}) copy-start(bf16[128,4,8,128]{0,3,2,1:T(8,128)(2,1)} %copy-done.3) | copy-start | bytes 3145732 | tf_op jit(solution)/shard_map/while
  130.2 209.6 %all-to-all-start = ((bf16[128,4,8,256]{0,3,1,2:T(8,128)(2,1)}), bf16[128,4,8,256]{0,3,1,2:T(8,128)(2,1)S(1)}, u32[]{:S(2)}, u32[]{:S(2)}) async-start(bf16[128,4,8,256]{0,3,1,2:T(8,128)(2,1)} %copy.78), calls=%async_computation.1 | async-start | bytes 4194304 | tf_op jit(solution)/shard_map/all_to_all | solution.py:113
  161.1 238.7 %reduce-scatter.5.cloned.1.call-start = ((), (), s32[]{:S(2)}) async-start(), calls=%async_computation.6 | async-start | bytes 5242880 | tf_op jit(solution)/shard_map/reduce_scatter | solution.py:121
  278.6 72.7 %copy-start.6 = (f32[128,1024]{1,0:T(8,128)S(1)}, f32[128,1024]{1,0:T(8,128)}, u32[]{:S(2)}) copy-start(f32[128,1024]{1,0:T(8,128)} %reduce-scatter.3.cloned.1.call-done) | copy-start | bytes 1572868
  279.7 10.8 %collective-permute-start = (bf16[128,1024]{1,0:T(8,128)(2,1)S(1)}, bf16[128,1024]{1,0:T(8,128)(2,1)S(1)}, u32[]{:S(2)}, u32[]{:S(2)}) collective-permute-start(bf16[128,1024]{1,0:T(8,128)(2,1)S(1)} %convert_element_type.17), channel_id=1, source_target_pairs={{0,1},{1,2},{2,3},{3,4},{4,5},{5,6},{6,7},{7,0},{8,9},{9,10},{10,1... | collective-permute-start | bytes 786440 | tf_op jit(solution)/shard_map/ppermute | solution.py:19
  290.6 9.9 %collective-permute-start.1 = (bf16[128,1024]{1,0:T(8,128)(2,1)S(1)}, bf16[128,1024]{1,0:T(8,128)(2,1)S(1)}, u32[]{:S(2)}, u32[]{:S(2)}) collective-permute-start(bf16[128,1024]{1,0:T(8,128)(2,1)S(1)} %collective-permute-done), channel_id=1, source_target_pairs={{0,1},{1,2},{2,3},{3,4},{4,5},{5,6},{6,7},{7,0},{8,9},{9,10},{10,1... | collective-permute-start | bytes 786440 | tf_op jit(solution)/shard_map/ppermute | solution.py:19
  300.5 9.1 %collective-permute-start.2 = (bf16[128,1024]{1,0:T(8,128)(2,1)S(1)}, bf16[128,1024]{1,0:T(8,128)(2,1)S(1)}, u32[]{:S(2)}, u32[]{:S(2)}) collective-permute-start(bf16[128,1024]{1,0:T(8,128)(2,1)S(1)} %collective-permute-done.1), channel_id=1, source_target_pairs={{0,1},{1,2},{2,3},{3,4},{4,5},{5,6},{6,7},{7,0},{8,9},{9,10},{10,1... | collective-permute-start | bytes 786440 | tf_op jit(solution)/shard_map/ppermute | solution.py:19
  309.5 0.7 copy-start.8
  310.2 9.1 %collective-permute-start.3 = (bf16[128,1024]{1,0:T(8,128)(2,1)S(1)}, bf16[128,1024]{1,0:T(8,128)(2,1)S(1)}, u32[]{:S(2)}, u32[]{:S(2)}) collective-permute-start(bf16[128,1024]{1,0:T(8,128)(2,1)S(1)} %collective-permute-done.2), channel_id=1, source_target_pairs={{0,1},{1,2},{2,3},{3,4},{4,5},{5,6},{6,7},{7,0},{8,9},{9,10},{10,1... | collective-permute-start | bytes 786440 | tf_op jit(solution)/shard_map/ppermute | solution.py:19
  319.3 0.7 copy-start.10
  320.0 9.1 %collective-permute-start.4 = (bf16[128,1024]{1,0:T(8,128)(2,1)S(1)}, bf16[128,1024]{1,0:T(8,128)(2,1)S(1)}, u32[]{:S(2)}, u32[]{:S(2)}) collective-permute-start(bf16[128,1024]{1,0:T(8,128)(2,1)S(1)} %collective-permute-done.3), channel_id=1, source_target_pairs={{0,1},{1,2},{2,3},{3,4},{4,5},{5,6},{6,7},{7,0},{8,9},{9,10},{10,1... | collective-permute-start | bytes 786440 | tf_op jit(solution)/shard_map/ppermute | solution.py:19
  329.1 0.7 copy-start.12
  329.8 10.0 %collective-permute-start.5 = (bf16[128,1024]{1,0:T(8,128)(2,1)S(1)}, bf16[128,1024]{1,0:T(8,128)(2,1)}, u32[]{:S(2)}, u32[]{:S(2)}) collective-permute-start(bf16[128,1024]{1,0:T(8,128)(2,1)S(1)} %collective-permute-done.4), channel_id=1, source_target_pairs={{0,1},{1,2},{2,3},{3,4},{4,5},{5,6},{6,7},{7,0},{8,9},{9,10},{10,1... | collective-permute-start | bytes 786440 | tf_op jit(solution)/shard_map/ppermute | solution.py:19
  339.8 9.4 %collective-permute-start.6 = (bf16[128,1024]{1,0:T(8,128)(2,1)}, bf16[128,1024]{1,0:T(8,128)(2,1)}, u32[]{:S(2)}, u32[]{:S(2)}) collective-permute-start(bf16[128,1024]{1,0:T(8,128)(2,1)} %collective-permute-done.5), channel_id=1, source_target_pairs={{0,1},{1,2},{2,3},{3,4},{4,5},{5,6},{6,7},{7,0},{8,9},{9,10},{10,1... | collective-permute-start | bytes 786440 | tf_op jit(solution)/shard_map/ppermute | solution.py:19
  339.8 11.3 %copy-start.13 = (bf16[128,1024]{1,0:T(8,128)(2,1)S(1)}, bf16[128,1024]{1,0:T(8,128)(2,1)}, u32[]{:S(2)}) copy-start(bf16[128,1024]{1,0:T(8,128)(2,1)} %copy-done.12) | copy-start | bytes 786436
  339.8 11.4 %copy-start.11 = (bf16[128,1024]{1,0:T(8,128)(2,1)S(1)}, bf16[128,1024]{1,0:T(8,128)(2,1)}, u32[]{:S(2)}) copy-start(bf16[128,1024]{1,0:T(8,128)(2,1)} %copy-done.10) | copy-start | bytes 786436
  339.8 11.4 %copy-start.9 = (bf16[128,1024]{1,0:T(8,128)(2,1)S(1)}, bf16[128,1024]{1,0:T(8,128)(2,1)}, u32[]{:S(2)}) copy-start(bf16[128,1024]{1,0:T(8,128)(2,1)} %copy-done.8) | copy-start | bytes 786436
  357.8 1.6 copy-start.2
Sparse Core Ops, SparseCore 0:
  10.6 42.2 all-gather.2
  55.5 38.4 all-gather.4
  125.6 152.9 reduce-scatter.2
  358.0 41.7 reduce-scatter.4
